TPU v7x, 32 devices: a whole 2x2x4 slice. The times are simulated.
32 devices in a mesh: dp: 2 (over core), row: 4 (over y, x), col: 4 (over z).
Axes of the slice: x: 2, y: 2, z: 4, core: 2. Of those that a mesh axis runs over, the one named last changes fastest.
Arguments:
- tokens: bfloat16 [1024, 768], P(('dp', 'col'), 'row'), may hold values from -150 to 150
- out_grad: bfloat16 [1024, 768], P(('dp', 'col'), 'row'), may hold values from -6 to 6
- segment_ids: int32 [2, 512], P('dp'), may hold values from 0 to 1, never falling along the last dimension, each value on 1 to 384 neighbouring positions
- w_qkv: bfloat16 [768, 2304], P('row', 'col'), may hold values from -8 to 8
- w_out: bfloat16 [768, 768], P('col', 'row'), may hold values from -0.875 to 0.875
- w_fc: bfloat16 [768, 3072], P('row', 'col'), may hold values from -0.21875 to 0.21875
- w_proj: bfloat16 [3072, 768], P('col', 'row'), may hold values from -0.109375 to 0.109375
- bias_qkv: float32 [2304], P('col'), may hold values from -1.8 to 1.8
- bias_fc: float32 [3072], P('col'), may hold values from -1.8 to 1.8
- row_vectors: float32 [6, 768], P(None, 'row'), may hold values from -0.6 to 1.5
- mom_qkv: float32 [768, 2304], P('row', 'col'), may hold values from -20 to 20
- mom_out: float32 [768, 768], P('col', 'row'), may hold values from -20 to 20
- mom_fc: float32 [768, 3072], P('row', 'col'), may hold values from -20 to 20
- mom_proj: float32 [3072, 768], P('col', 'row'), may hold values from -20 to 20
- mom_bias_qkv: float32 [2304], P('col'), may hold values from -20 to 20
- mom_bias_fc: float32 [3072], P('col'), may hold values from -20 to 20
- mom_rows: float32 [6, 768], P(None, 'row'), may hold values from -20 to 20
Outputs:
- block_out: bfloat16 [1024, 768], P(('dp', 'col'), 'row')
- input_grad: float32 [1024, 768], P(('dp', 'col'), 'row')
- grad_qkv: float32 [768, 2304], P('row', 'col')
- grad_out: float32 [768, 768], P('col', 'row')
- grad_fc: float32 [768, 3072], P('row', 'col')
- grad_proj: float32 [3072, 768], P('col', 'row')
- grad_bias_qkv: float32 [2304], P('col')
- grad_bias_fc: float32 [3072], P('col')
- grad_rows: float32 [6, 768], P(None, 'row')
- new_qkv: float32 [768, 2304], P('row', 'col')
- new_out: float32 [768, 768], P('col', 'row')
- new_fc: float32 [768, 3072], P('row', 'col')
- new_proj: float32 [3072, 768], P('col', 'row')
- new_bias_qkv: float32 [2304], P('col')
- new_bias_fc: float32 [3072], P('col')
- new_rows: float32 [6, 768], P(None, 'row')
- new_mom_qkv: float32 [768, 2304], P('row', 'col')
- new_mom_out: float32 [768, 768], P('col', 'row')
- new_mom_fc: float32 [768, 3072], P('row', 'col')
- new_mom_proj: float32 [3072, 768], P('col', 'row')
- new_mom_bias_qkv: float32 [2304], P('col')
- new_mom_bias_fc: float32 [3072], P('col')
- new_mom_rows: float32 [6, 768], P(None, 'row')
Inputs may be any that keep to these rules, and one draw needn't show every extreme that they name: `segment_ids`: within each data group the segment numbers never fall; the group's 2 sequences have 512 tokens together, each at most 384.
All inputs are finite; a program needn't handle non-finite values.
Results may differ from a plain program's by a relative error of at most 0.012.
Values may be sent and summed in bfloat16 or wider, within the bound.
A program may use at most 128 MiB of HBM per device.

v0:
```python
import math
import jax
import jax.numpy as jnp
from jax import lax
from jax.sharding import PartitionSpec as P

HD = 64
NS_STEPS = 2
eps_norm = 1e-05
eps_gram = 1e-06
coef_a = 3.4445
coef_b = -4.775
coef_c = 2.0315
beta_mom = 0.95
rate_matrix = 0.03
rate_vector = 0.6


def gelu_value(values):
    return jax.nn.gelu(values, approximate=True)


def gelu_slope(values):
    return jax.vjp(gelu_value, values)[1](jnp.ones_like(values))[0]


def product(left_side, right_side, flip_right):
    if flip_right:
        return lax.dot_general(
            left_side, right_side, (((1,), (1,)), ((), ())), preferred_element_type=jnp.float32
        )
    return jnp.dot(left_side, right_side, preferred_element_type=jnp.float32)


def inner_rows(left_side, right_side):
    return lax.dot_general(
        left_side, right_side, (((0,), (0,)), ((), ())), preferred_element_type=jnp.float32
    )


def tile_grid(blocks, first_parts, second_parts):
    height = blocks.shape[1]
    breadth = blocks.shape[2]
    tiled = blocks.reshape(first_parts, second_parts, height, breadth)
    return tiled.transpose(0, 2, 1, 3).reshape(first_parts * height, second_parts * breadth)


def gather_grid(local_piece):
    blocks = lax.all_gather(local_piece, ("col", "row"), axis=0, tiled=False)
    return tile_grid(
        blocks.reshape((-1,) + local_piece.shape), lax.axis_size("col"), lax.axis_size("row")
    )


def norm_stats(values):
    mean_row = jnp.mean(values, axis=1, keepdims=True)
    square = jnp.mean(values * values, axis=1, keepdims=True)
    inv_std = lax.rsqrt(square - mean_row * mean_row + eps_norm)
    return (mean_row, inv_std)


def matrix_product(left_side, right_side):
    return jnp.dot(
        left_side.astype(jnp.bfloat16),
        right_side.astype(jnp.bfloat16),
        preferred_element_type=jnp.float32,
    )


def polynomial_factor(gram_matrix):
    gram_norm = jnp.sqrt(jnp.sum(gram_matrix * gram_matrix)) + eps_gram
    gram_now = gram_matrix / gram_norm
    poly_before = None
    for repeat in range(NS_STEPS):
        poly = coef_b * gram_now + coef_c * matrix_product(gram_now, gram_now)
        if poly_before is None:
            factor = poly
            scale = coef_a
        else:
            factor = coef_a * factor + scale * poly + matrix_product(poly, factor)
            scale = scale * coef_a
        if repeat + 1 < NS_STEPS:
            half = coef_a * gram_now + matrix_product(poly, gram_now)
            gram_now = coef_a * half + matrix_product(half, poly)
        poly_before = poly
    return (factor, scale, gram_norm)


def local(
    tokens,
    out_grad,
    segment_ids,
    w_qkv,
    w_out,
    w_fc,
    w_proj,
    bias_qkv,
    bias_fc,
    row_vectors,
    mom_qkv,
    mom_out,
    mom_fc,
    mom_proj,
    mom_bias_qkv,
    mom_bias_fc,
    mom_rows,
):
    low = jnp.bfloat16
    score_scale = 1.0 / math.sqrt(HD)
    row_parts = lax.axis_size("row")
    col_parts = lax.axis_size("col")
    dp_parts = lax.axis_size("dp")
    own_tokens, own_features = tokens.shape
    token_count = own_tokens * col_parts
    feature_count = own_features * row_parts
    token_base = lax.axis_index("col") * own_tokens
    feature_base = lax.axis_index("row") * own_features

    def own_columns(whole):
        return lax.dynamic_slice_in_dim(whole, feature_base, own_features, 1)

    def own_block(whole):
        return lax.dynamic_slice(whole, (token_base, feature_base), (own_tokens, own_features))

    def own_rows(whole):
        return lax.dynamic_slice_in_dim(whole, token_base, own_tokens, 0)

    tokens_all = gather_grid(tokens)
    qkv_cols = lax.all_gather(w_qkv, "row", axis=0, tiled=True)
    vectors_all = lax.all_gather(row_vectors, "row", axis=1, tiled=True)
    out_whole = gather_grid(w_out)
    fc_cols = lax.all_gather(w_fc, "row", axis=0, tiled=True)
    grad_all = gather_grid(out_grad)
    proj_flip = w_proj.T
    proj_cols = lax.all_gather(proj_flip, "row", axis=0, tiled=True)
    gain_one, shift_one, gain_two, shift_two, bias_out, _ = [
        vectors_all[which] for which in range(6)
    ]
    resid_in = tokens_all.astype(jnp.float32)
    mean_one, inv_one = norm_stats(resid_in)
    unit_one = (resid_in - mean_one) * inv_one
    act_one = (unit_one * gain_one + shift_one).astype(low)
    qkv_local = (product(act_one, qkv_cols, False) + bias_qkv).astype(low)
    heads_local = qkv_local.shape[1] // (3 * HD)
    qkv_tiles = qkv_local.reshape(token_count, heads_local, 3, HD).transpose(2, 1, 0, 3)
    query, key, value = (qkv_tiles[0], qkv_tiles[1], qkv_tiles[2])
    segment_row = segment_ids[0]
    positions = jnp.arange(token_count, dtype=jnp.int32)
    allowed = (positions[None, :] <= positions[:, None]) & (
        segment_row[None, :] == segment_row[:, None]
    )
    scores = (
        jnp.einsum("hqe,hke->hqk", query, key, preferred_element_type=jnp.float32) * score_scale
    )
    scores = jnp.where(allowed[None], scores, -jnp.inf)
    row_max = jnp.max(scores, axis=2, keepdims=True)
    raised = jnp.exp(scores - row_max)
    probs = raised / jnp.sum(raised, axis=2, keepdims=True)
    prob_low = probs.astype(low)
    attended = jnp.einsum(
        "hqk,hke->hqe", prob_low, value, preferred_element_type=jnp.float32
    ).astype(low)
    attn_local = attended.transpose(1, 0, 2).reshape(token_count, heads_local * HD)
    attn_all = lax.all_gather(attn_local, "col", axis=1, tiled=True)
    resid_mid = resid_in + product(attn_all, out_whole, False) + bias_out
    mean_two, inv_two = norm_stats(resid_mid)
    unit_two = (resid_mid - mean_two) * inv_two
    act_two = (unit_two * gain_two + shift_two).astype(low)
    hidden_pre = product(act_two, fc_cols, False) + bias_fc
    hidden = gelu_value(hidden_pre).astype(low)
    grad_hidden = product(grad_all, proj_cols, False)
    grad_pre = (gelu_slope(hidden_pre) * grad_hidden).astype(low)
    grad_norm_two = lax.psum_scatter(
        product(grad_pre, w_fc, True).astype(low), "col", scatter_dimension=0, tiled=True
    )
    grad_two_all = gather_grid(grad_norm_two).astype(jnp.float32)
    grad_norm_two = grad_norm_two.astype(jnp.float32)
    scaled = grad_two_all * gain_two
    first_mean = jnp.mean(scaled, axis=1, keepdims=True)
    second_mean = jnp.mean(scaled * unit_two, axis=1, keepdims=True)
    grad_mid_all = grad_all.astype(jnp.float32) + inv_two * (
        scaled - first_mean - unit_two * second_mean
    )
    grad_mid_low = grad_mid_all.astype(low)
    out_rows = lax.dynamic_slice_in_dim(
        out_whole, lax.axis_index("col") * w_out.shape[0], w_out.shape[0], 0
    )
    grad_attn = (
        product(grad_mid_low, out_rows, True)
        .astype(low)
        .reshape(token_count, heads_local, HD)
        .transpose(1, 0, 2)
    )
    grad_value = jnp.einsum("hqk,hqe->hke", prob_low, grad_attn, preferred_element_type=jnp.float32)
    grad_probs = jnp.einsum("hqe,hke->hqk", grad_attn, value, preferred_element_type=jnp.float32)
    row_dot = jnp.sum(
        grad_attn.astype(jnp.float32) * attended.astype(jnp.float32), axis=2, keepdims=True
    )
    grad_scores = (score_scale * probs * (grad_probs - row_dot)).astype(low)
    grad_query = jnp.einsum("hqk,hke->hqe", grad_scores, key, preferred_element_type=jnp.float32)
    grad_key = jnp.einsum("hqk,hqe->hke", grad_scores, query, preferred_element_type=jnp.float32)
    grad_qkv_low = (
        jnp.stack([grad_query.astype(low), grad_key.astype(low), grad_value.astype(low)], axis=0)
        .transpose(2, 1, 0, 3)
        .reshape(token_count, heads_local * 3 * HD)
    )
    grad_blocks = (
        inner_rows(own_columns(act_one), grad_qkv_low),
        inner_rows(attn_local, own_columns(grad_mid_low)),
        inner_rows(own_columns(act_two), grad_pre),
        inner_rows(hidden, own_columns(grad_all)),
    )
    summed = [lax.psum(block.astype(low), "dp").astype(jnp.float32) for block in grad_blocks]
    bias_sums = lax.psum(
        (
            jnp.sum(grad_qkv_low, axis=0, dtype=jnp.float32),
            jnp.sum(grad_pre, axis=0, dtype=jnp.float32),
        ),
        "dp",
    )
    summed = summed + list(bias_sums)
    weights = (w_qkv, w_out, w_fc, w_proj)
    moments = (mom_qkv, mom_out, mom_fc, mom_proj)
    flips = (False, True, False, True)
    new_moms = [beta_mom * moments[member] + summed[member] for member in range(4)]
    pushes = [(summed[member] + beta_mom * new_moms[member]).astype(low) for member in range(4)]
    upright = [pushes[member].T if flips[member] else pushes[member] for member in range(4)]
    widest = max((piece.shape[1] for piece in upright))
    share = -(-widest // dp_parts)
    assert row_parts == len(upright)
    outgoing = jnp.stack(
        [jnp.pad(piece, ((0, 0), (0, share * dp_parts - piece.shape[1]))) for piece in upright]
    )
    outgoing = lax.dynamic_slice_in_dim(outgoing, lax.axis_index("dp") * share, share, 2)
    arrived = lax.all_to_all(outgoing, "row", split_axis=0, concat_axis=0, tiled=True)
    matrix = arrived.reshape(feature_count, share)
    gram = lax.psum(product(matrix, matrix, True).astype(low), ("dp", "col")).astype(jnp.float32)
    factor, scale, gram_norm = polynomial_factor(gram)
    ortho = (scale * matrix.astype(jnp.float32) + matrix_product(factor, matrix)) * lax.rsqrt(
        gram_norm
    )
    back = lax.all_to_all(
        ortho.astype(low).reshape(row_parts, own_features, share),
        "row",
        split_axis=0,
        concat_axis=0,
        tiled=True,
    )
    orthos = lax.all_gather(back, "dp", axis=2, tiled=True)
    new_weights = []
    for member in range(4):
        piece = orthos[member, :, : upright[member].shape[1]]
        if flips[member]:
            piece = piece.T
        longest = max(upright[member].shape[0] * row_parts, upright[member].shape[1] * col_parts)
        new_weights.append(
            weights[member].astype(jnp.float32)
            - rate_matrix * math.sqrt(longest) * piece.astype(jnp.float32)
        )
    block_sum = lax.psum_scatter(
        product(hidden, proj_flip, True).astype(low), "col", scatter_dimension=0, tiled=True
    ).astype(jnp.float32)
    block_out = (own_block(resid_mid) + block_sum + row_vectors[5]).astype(low)
    grad_norm_one = lax.psum_scatter(
        product(grad_qkv_low, w_qkv, True).astype(low), "col", scatter_dimension=0, tiled=True
    ).astype(jnp.float32)
    unit_one_own = own_block(unit_one)
    scaled_one = grad_norm_one * row_vectors[0]
    first_sum, second_sum = lax.psum(
        (
            jnp.sum(scaled_one, axis=1, keepdims=True),
            jnp.sum(scaled_one * unit_one_own, axis=1, keepdims=True),
        ),
        "row",
    )
    input_grad = own_block(grad_mid_all) + own_rows(inv_one) * (
        scaled_one - first_sum / feature_count - unit_one_own * (second_sum / feature_count)
    )
    row_terms = jnp.stack(
        [
            jnp.sum(grad_norm_one * unit_one_own, axis=0),
            jnp.sum(grad_norm_one, axis=0),
            jnp.sum(grad_norm_two * own_block(unit_two), axis=0),
            jnp.sum(grad_norm_two, axis=0),
            jnp.sum(own_block(grad_mid_low), axis=0, dtype=jnp.float32),
            jnp.sum(out_grad, axis=0, dtype=jnp.float32),
        ]
    )
    grad_rows = lax.psum(row_terms, ("dp", "col"))
    vector_rate = rate_vector / math.sqrt(token_count * dp_parts)

    def vector_step(weight, gradient, moment):
        new_moment = beta_mom * moment + gradient
        return (weight - vector_rate * (gradient + beta_mom * new_moment), new_moment)

    new_bias_qkv, new_mom_bias_qkv = vector_step(bias_qkv, summed[4], mom_bias_qkv)
    new_bias_fc, new_mom_bias_fc = vector_step(bias_fc, summed[5], mom_bias_fc)
    new_rows, new_mom_rows = vector_step(row_vectors, grad_rows, mom_rows)
    return (
        block_out,
        input_grad,
        summed[0],
        summed[1],
        summed[2],
        summed[3],
        summed[4],
        summed[5],
        grad_rows,
        new_weights[0],
        new_weights[1],
        new_weights[2],
        new_weights[3],
        new_bias_qkv,
        new_bias_fc,
        new_rows,
        new_moms[0],
        new_moms[1],
        new_moms[2],
        new_moms[3],
        new_mom_bias_qkv,
        new_mom_bias_fc,
        new_mom_rows,
    )


def solution(mesh):
    placed = (
        P(("dp", "col"), "row"),
        P(("dp", "col"), "row"),
        P("dp", None),
        P("row", "col"),
        P("col", "row"),
        P("row", "col"),
        P("col", "row"),
        P("col"),
        P("col"),
        P(None, "row"),
        P("row", "col"),
        P("col", "row"),
        P("row", "col"),
        P("col", "row"),
        P("col"),
        P("col"),
        P(None, "row"),
    )
    return jax.shard_map(
        local,
        mesh=mesh,
        in_specs=placed,
        out_specs=(
            P(("dp", "col"), "row"),
            P(("dp", "col"), "row"),
            P("row", "col"),
            P("col", "row"),
            P("row", "col"),
            P("col", "row"),
            P("col"),
            P("col"),
            P(None, "row"),
            P("row", "col"),
            P("col", "row"),
            P("row", "col"),
            P("col", "row"),
            P("col"),
            P("col"),
            P(None, "row"),
            P("row", "col"),
            P("col", "row"),
            P("row", "col"),
            P("col", "row"),
            P("col"),
            P("col"),
            P(None, "row"),
        ),
        check_vma=False,
    )
```

profile of v0, /device:TPU:0, one launch (start us, length us, event | category | flops | bytes accessed | tf_op | source)
XLA Modules:
  0.0 442.9 jit_solution(18156364736476720442)
XLA Ops:
  9.5 47.6 %all-gather = bf16[2048,192]{0,1:T(8,128)(2,1)S(1)} all-gather(bf16[128,192]{0,1:T(8,128)(2,1)} %param.17), channel_id=2, replica_groups=mesh['dp'=2,'row'=4,'col'=4] {'col','row'}, dimensions={0}, use_global_device_ids=true | all-gather | bytes 835584 | tf_op jit(solution)/shard_map/all_gather | solution.py:49
  60.2 6.9 %all-gather.4 = f32[4,192,6]{1,2,0:T(8,128)S(1)} all-gather(f32[1,192,6]{1,2,0:T(8,128)S(1)} %bitcast.210), channel_id=1, replica_groups=mesh['dp'=2,'row'=4,'col'=4] {'row'}, dimensions={0}, use_global_device_ids=true | all-gather | bytes 23040 | tf_op jit(solution)/shard_map/all_gather | solution.py:130
  69.0 13.3 %all_gather.45 = bf16[768,576]{1,0:T(8,128)(2,1)S(1)} all-gather(bf16[192,576]{1,0:T(8,128)(2,1)S(1)} %copy-done.16), channel_id=1, replica_groups=mesh['dp'=2,'row'=4,'col'=4] {'row'}, dimensions={0}, use_global_device_ids=true | all-gather | bytes 1105920 | tf_op jit(solution)/shard_map/all_gather | solution.py:129
  85.5 43.6 %all-gather.2 = bf16[2048,192]{0,1:T(8,128)(2,1)S(1)} all-gather(bf16[128,192]{0,1:T(8,128)(2,1)S(1)} %copy-done.30), channel_id=4, replica_groups=mesh['dp'=2,'row'=4,'col'=4] {'col','row'}, dimensions={0}, use_global_device_ids=true | all-gather | bytes 835584 | tf_op jit(solution)/shard_map/all_gather | solution.py:49
  131.5 4.1 fusion.73
  139.4 16.6 %all_gather.46 = bf16[512,768]{0,1:T(8,128)(2,1)} all-gather(bf16[512,192]{0,1:T(8,128)(2,1)S(1)} %bitcast.195), channel_id=1, replica_groups=mesh['dp'=2,'row'=4,'col'=4] {'col'}, dimensions={1}, use_global_device_ids=true | all-gather | bytes 983040 | tf_op jit(solution)/shard_map/all_gather | solution.py:164
  156.0 3.9 copy.219
  159.9 3.1 reshape.253
  163.0 2.6 fusion.70
  168.0 3.8 multiply_convert_fusion.1
  171.9 4.2 convert_reduce_fusion
  182.8 12.3 %reduce-scatter.12.cloned.1.call-done = bf16[128,192]{1,0:T(8,128)(2,1)} async-done(((bf16[512,192]{1,0:T(8,128)(2,1)}), bf16[128,192]{1,0:T(8,128)(2,1)}) %reduce-scatter.12.cloned.1.call-update) | async-done | bytes 49168 | tf_op jit(solution)/shard_map/reduce_scatter | solution.py:173
  196.0 44.7 %all-gather.3 = bf16[2048,192]{0,1:T(8,128)(2,1)} all-gather(bf16[128,192]{0,1:T(8,128)(2,1)S(1)} %copy.201), channel_id=5, replica_groups=mesh['dp'=2,'row'=4,'col'=4] {'col','row'}, dimensions={0}, use_global_device_ids=true | all-gather | bytes 835584 | tf_op jit(solution)/shard_map/all_gather | solution.py:49
  244.7 3.1 copy.174
  260.4 15.7 %all-reduce.10.cloned.1.call-done = (bf16[192,192]{0,1:T(8,128)(2,1)}, bf16[192,576]{1,0:T(8,128)(2,1)}, bf16[192,768]{1,0:T(8,128)(2,1)}, bf16[768,192]{0,1:T(8,128)(2,1)}) async-done(((bf16[192,192]{0,1:T(8,128)(2,1)}, bf16[192,576]{1,0:T(8,128)(2,1)}, bf16[192,768]{1,0:T(8,128)(2,1)}, bf16[768,192]{0,1:T(8,128)(2,1)}), (bf16[192,192]{0,1:T(8,128)(2,1)}, bf16[192,576]{1,0:T(8,128)(2,1)}, ...) | async-done | bytes 884752 | tf_op jit(solution)/shard_map/psum | solution.py:213
  281.7 13.6 %all_to_all.10 = bf16[4,192,384]{2,1,0:T(8,128)(2,1)S(1)} all-to-all(bf16[4,192,384]{2,1,0:T(8,128)(2,1)S(1)} %fusion.34), channel_id=1, replica_groups=mesh['dp'=2,'row'=4,'col'=4] {'row'}, dimensions={0} | all-to-all | bytes 1179648 | tf_op jit(solution)/shard_map/all_to_all | solution.py:235
  305.9 50.5 %all-reduce.8.cloned.1.call-done = bf16[768,768]{1,0:T(8,128)(2,1)} async-done(((bf16[768,768]{1,0:T(8,128)(2,1)}), bf16[768,768]{1,0:T(8,128)(2,1)}) %all-reduce.8.cloned.1.call-update) | async-done | bytes 1179664 | tf_op jit(solution)/shard_map/psum | solution.py:237
  359.6 3.4 multiply_add_fusion.4
  368.1 6.3 %fusion.18 = bf16[768,384]{1,0:T(8,128)(2,1)} fusion(bf16[768,384]{1,0:T(8,128)(2,1)S(1)} %bitcast.188, f32[768,768]{1,0:T(8,128)} %copy-done.13, f32[768,768]{1,0:T(8,128)} %multiply_add_fusion.1, f32[]{:T(128)S(6)} %rsqrt.28), kind=kOutput, calls=%fused_computation.51 | convolution fusion | flops 1363968000 | bytes 5898244 | tf_op jit(solution)/shard_map/dot_general | solution.py:63
  374.5 3.8 all-to-all-start.1
  381.0 2.6 all-reduce.3
  388.3 11.0 %reduce-scatter.14.cloned.1.call-done = bf16[128,192]{1,0:T(8,128)(2,1)} async-done(((bf16[512,192]{1,0:T(8,128)(2,1)}), bf16[128,192]{1,0:T(8,128)(2,1)}) %reduce-scatter.14.cloned.1.call-update) | async-done | bytes 49168 | tf_op jit(solution)/shard_map/reduce_scatter | solution.py:264
  400.5 9.9 %all-reduce.2 = (f32[128,1]{0,1:T(1,128)S(1)}, f32[128,1]{0,1:T(1,128)S(1)}) all-reduce(f32[128,1]{0,1:T(1,128)S(1)} %bitcast.222, f32[128,1]{0,1:T(1,128)S(1)} %bitcast.223), channel_id=1, replica_groups=mesh['dp'=2,'row'=4,'col'=4] {'row'}, use_global_device_ids=true, to_apply=%region_15.16 | all-reduce | flops 256 | bytes 2048 | tf_op jit(solution)/shard_map/psum | solution.py:269
  412.4 14.4 %psum.78 = f32[6,192]{1,0:T(8,128)S(1)} all-reduce(f32[6,192]{1,0:T(8,128)S(1)} %stack.58), channel_id=1, replica_groups=mesh['dp'=2,'row'=4,'col'=4] {'dp','col'}, use_global_device_ids=true, to_apply=%region_30.31 | all-reduce | flops 1152 | bytes 9216 | tf_op jit(solution)/shard_map/psum | solution.py:289
  (202 shorter events, 86.7 us)
Async XLA Ops:
  7.2 148.8 %all-gather.16.cloned.1.call-start = ((), (), s32[]{:S(2)}) async-start(), calls=%async_computation.9 | async-start | bytes 1671168 | tf_op jit(solution)/shard_map/all_gather | solution.py:49
  7.9 160.1 %all-gather.10.cloned.1.call-start = ((), (), s32[]{:S(2)}) async-start(), calls=%async_computation.5 | async-start | bytes 1474560 | tf_op jit(solution)/shard_map/all_gather | solution.py:132
  8.7 163.2 %all-gather.12.cloned.1.call-start = ((), (), s32[]{:S(2)}) async-start(), calls=%async_computation.6 | async-start | bytes 1474560 | tf_op jit(solution)/shard_map/all_gather | solution.py:135
  9.4 185.6 %reduce-scatter.12.cloned.1.call-start = ((), (), s32[]{:S(2)}) async-start(), calls=%async_computation.11 | async-start | bytes 327680 | tf_op jit(solution)/shard_map/reduce_scatter | solution.py:173
  137.9 22.0 %copy-start.1 = (bf16[3,512,512]{1,2,0:T(8,128)(2,1)}, bf16[3,512,512]{1,2,0:T(8,128)(2,1)S(1)}, u32[]{:S(2)}) copy-start(bf16[3,512,512]{1,2,0:T(8,128)(2,1)S(1)} %fusion.19) | copy-start | bytes 4718596
  178.3 97.8 %all-reduce.10.cloned.1.call-start = ((), (), s32[]{:S(2)}) async-start(), calls=%async_computation.13 | async-start | bytes 1867776 | tf_op jit(solution)/shard_map/psum | solution.py:213
  260.2 96.2 %all-reduce.8.cloned.1.call-start = ((), (), s32[]{:S(2)}) async-start(), calls=%async_computation.7 | async-start | bytes 2359296 | tf_op jit(solution)/shard_map/psum | solution.py:237
  297.1 86.5 %reduce-scatter.10.cloned.1.call-start = ((), (), s32[]{:S(2)}) async-start(), calls=%async_computation.10 | async-start | bytes 327680 | tf_op jit(solution)/shard_map/reduce_scatter | solution.py:260
  301.2 98.1 %reduce-scatter.14.cloned.1.call-start = ((), (), s32[]{:S(2)}) async-start(), calls=%async_computation.12 | async-start | bytes 327680 | tf_op jit(solution)/shard_map/reduce_scatter | solution.py:264
  374.4 11.7 %copy-start.38 = (f32[576]{0:T(1024)S(1)}, f32[576]{0:T(1024)}, u32[]{:S(2)}) copy-start(f32[576]{0:T(1024)} %param.24) | copy-start | bytes 6916
  374.4 11.7 %copy-start.39 = (f32[576]{0:T(1024)S(1)}, f32[576]{0:T(1024)}, u32[]{:S(2)}) copy-start(f32[576]{0:T(1024)} %param.31) | copy-start | bytes 6916
  374.4 13.1 %copy-start.29 = (bf16[128,192]{1,0:T(8,128)(2,1)S(1)}, bf16[128,192]{1,0:T(8,128)(2,1)}, u32[]{:S(2)}) copy-start(bf16[128,192]{1,0:T(8,128)(2,1)} %reduce-scatter.12.cloned.1.call-done) | copy-start | bytes 147460
  374.4 13.3 %copy-start.41 = (f32[768]{0:T(1024)S(1)}, f32[768]{0:T(1024)}, u32[]{:S(2)}) copy-start(f32[768]{0:T(1024)} %param.25) | copy-start | bytes 9220
  374.4 13.3 %copy-start.42 = (f32[768]{0:T(1024)S(1)}, f32[768]{0:T(1024)}, u32[]{:S(2)}) copy-start(f32[768]{0:T(1024)} %param.32) | copy-start | bytes 9220
  374.5 24.9 %copy-start.34 = (f32[1,192]{1,0:T(1,128)S(1)}, f32[1,192]{1,0:T(1,128)}, u32[]{:S(2)}) copy-start(f32[1,192]{1,0:T(1,128)} %get-tuple-element.209) | copy-start | bytes 2308
  374.5 52.4 %copy-start.36 = (f32[6,192]{1,0:T(8,128)S(1)}, f32[6,192]{1,0:T(8,128)}, u32[]{:S(2)}) copy-start(f32[6,192]{1,0:T(8,128)} %param.33) | copy-start | bytes 13828
  374.5 10.8 %all-to-all-start.1 = ((bf16[4,192,384]{2,1,0:T(8,128)(2,1)}), bf16[4,192,384]{2,1,0:T(8,128)(2,1)S(1)}, u32[]{:S(2)}, u32[]{:S(2)}) async-start(bf16[4,192,384]{2,1,0:T(8,128)(2,1)} %bitcast.207), calls=%async_computation.1 | async-start | bytes 1179648 | tf_op jit(solution)/shard_map/all_to_all | solution.py:242
  378.2 49.2 %copy-start.26 = (bf16[192,192]{0,1:T(8,128)(2,1)S(1)}, bf16[192,192]{0,1:T(8,128)(2,1)}, u32[]{:S(2)}) copy-start(bf16[192,192]{0,1:T(8,128)(2,1)} %get-tuple-element.180) | copy-start | bytes 221188
  378.3 50.0 %copy-start.22 = (f32[192,192]{0,1:T(8,128)S(1)}, f32[192,192]{0,1:T(8,128)}, u32[]{:S(2)}) copy-start(f32[192,192]{0,1:T(8,128)} %get-tuple-element.207) | copy-start | bytes 442372
  378.3 50.8 %all-gather.14.cloned.1.call-start = ((), (), s32[]{:S(2)}) async-start(), calls=%async_computation.8 | async-start | bytes 1769472 | tf_op jit(solution)/shard_map/all_gather | solution.py:249
  383.6 46.4 %copy-start.43 = (f32[576]{0:T(1024)}, f32[576]{0:T(1024)S(1)}, u32[]{:S(2)}) copy-start(f32[576]{0:T(1024)S(1)} %get-tuple-element.178) | copy-start | bytes 6916
  383.6 46.4 %copy-start.44 = (f32[768]{0:T(1024)}, f32[768]{0:T(1024)S(1)}, u32[]{:S(2)}) copy-start(f32[768]{0:T(1024)S(1)} %get-tuple-element.179) | copy-start | bytes 9220
  386.1 44.7 %copy-start.17 = (bf16[192,576]{1,0:T(8,128)(2,1)S(1)}, bf16[192,576]{1,0:T(8,128)(2,1)}, u32[]{:S(2)}) copy-start(bf16[192,576]{1,0:T(8,128)(2,1)} %param.20) | copy-start | bytes 663556
  410.4 22.2 %copy-start.11 = (bf16[192,768]{1,0:T(8,128)(2,1)S(1)}, bf16[192,768]{1,0:T(8,128)(2,1)}, u32[]{:S(2)}) copy-start(bf16[192,768]{1,0:T(8,128)(2,1)} %param.22) | copy-start | bytes 884740
  (31 other events, 81.7 us)
Sparse Core Ops, SparseCore 0:
  10.8 64.3 all-gather.15
  77.0 32.6 all-gather.9
  111.6 27.0 all-gather.11
  178.4 16.5 reduce-scatter.11
  260.3 15.7 all-reduce.9
  297.2 59.0 all-reduce.7
  359.2 19.0 reduce-scatter.9
  381.1 18.2 reduce-scatter.13
  401.5 7.4 all-gather.13
where the time goes:
time: 444 us; the launch traced here: 443 us
  blocking collectives  213 us (48%)
  waiting for transfers between devices  92.2 us (21%)
  matrix products  49.5 us (11%)
  local copies, waits for them, and re-layouts  36.4 us (8%)
  other arithmetic  32 us (7%)
  between operations  15.2 us (3%)
    all_gather x3, blocking collectives, gather_grid(): blocks = lax.all_gather(local_piece, ('col', 'row'), axis=0, tiled=False)  136 us
    psum x1, waiting for transfers between devices, local(): lax.psum(product(matrix, matrix, True).astype(low), ('dp', 'col'))  50.5 us
    unnamed x105, local copies, waits for them, and re-layouts  16.8 us
    all_gather x1, blocking collectives, local(): attn_all = lax.all_gather(attn_local, 'col', axis=1, tiled=True)  16.6 us
    psum x1, waiting for transfers between devices, local(): lax.psum(block.astype(low), 'dp').astype(jnp.float32)  15.7 us
    dot_general x5, matrix products, matrix_product(): jnp.dot(left_side.astype(jnp.bfloat16), right_side.astype(jnp.bfloat16),...  14.5 us
    psum x1, blocking collectives, local(): grad_rows = lax.psum(row_terms, ('dp', 'col'))  14.4 us
    all_to_all x1, blocking collectives, local(): lax.all_to_all(outgoing, 'row', split_axis=0, concat_axis=0, tiled=True)  13.6 us
  transfers between devices with their start and end apart: 10, of which 5 were waited for; matrix products, arithmetic and copies ran while one was open for 17% of the time, Pallas kernels for 0%

commit v1 on v0

--- a/solution.py
+++ b/solution.py
@@ -234,7 +234,9 @@
     outgoing = lax.dynamic_slice_in_dim(outgoing, lax.axis_index("dp") * share, share, 2)
     arrived = lax.all_to_all(outgoing, "row", split_axis=0, concat_axis=0, tiled=True)
     matrix = arrived.reshape(feature_count, share)
-    gram = lax.psum(product(matrix, matrix, True).astype(low), ("dp", "col")).astype(jnp.float32)
+    gram = jnp.sum(
+        lax.all_gather(product(matrix, matrix, True).astype(low), ("dp", "col")), axis=0
+    ).astype(jnp.float32)
     factor, scale, gram_norm = polynomial_factor(gram)
     ortho = (scale * matrix.astype(jnp.float32) + matrix_product(factor, matrix)) * lax.rsqrt(
         gram_norm

time: 444 us -> 472 us (1.063)
  waiting for transfers between devices: 92.2 us -> 120 us
    all_gather x0 -> x1, waiting for transfers between devices: none -> 83.8 us  [local(): lax.all_gather(product(matrix, matrix, True).astype(low), ('dp', 'col'))]
    psum x1 -> x0, waiting for transfers between devices: 50.5 us -> none  [local(): lax.psum(product(matrix, matrix, True).astype(low), ('dp', 'col'))]
    reduce_scatter x1, waiting for transfers between devices: 11 us -> 2.17 us  [local(): lax.psum_scatter(product(grad_qkv_low, w_qkv, True).astype(low), 'col', s...]
    reduce_sum x0 -> x1, other arithmetic: none -> 5.71 us  [local(): jnp.sum(lax.all_gather(product(matrix, matrix, True).astype(low), ('dp',...]
    unnamed x105 -> x113, local copies, waits for them, and re-layouts: 16.8 us -> 14.7 us
  transfers between devices with their start and end apart: 10 -> 10, of which waited for: 5 -> 5; matrix products, arithmetic and copies ran while one was open for 17% -> 16% of each run, Pallas kernels for 0% -> 0%
where the time goes in v1:
time: 472 us; the launch traced here: 471 us
  blocking collectives  213 us (45%)
  waiting for transfers between devices  120 us (25%)
  matrix products  49.7 us (11%)
  other arithmetic  34.7 us (7%)
  local copies, waits for them, and re-layouts  33.6 us (7%)
  between operations  15.2 us (3%)
    all_gather x3, blocking collectives, gather_grid(): blocks = lax.all_gather(local_piece, ('col', 'row'), axis=0, tiled=False)  136 us
    all_gather x1, waiting for transfers between devices, local(): lax.all_gather(product(matrix, matrix, True).astype(low), ('dp', 'col'))  83.8 us
    all_gather x1, blocking collectives, local(): attn_all = lax.all_gather(attn_local, 'col', axis=1, tiled=True)  16.6 us
    dot_general x5, matrix products, matrix_product(): jnp.dot(left_side.astype(jnp.bfloat16), right_side.astype(jnp.bfloat16),...  15.5 us
    psum x1, waiting for transfers between devices, local(): lax.psum(block.astype(low), 'dp').astype(jnp.float32)  15.3 us
    unnamed x113, local copies, waits for them, and re-layouts  14.7 us
    psum x1, blocking collectives, local(): grad_rows = lax.psum(row_terms, ('dp', 'col'))  14.5 us
    all_to_all x1, blocking collectives, local(): lax.all_to_all(outgoing, 'row', split_axis=0, concat_axis=0, tiled=True)  13.6 us
  transfers between devices with their start and end apart: 10, of which 5 were waited for; matrix products, arithmetic and copies ran while one was open for 16% of the time, Pallas kernels for 0%

profile of v1, /device:TPU:0, one launch (start us, length us, event | category | flops | bytes accessed | tf_op | source)
XLA Modules:
  0.0 470.9 jit_solution(6001297975162511623)
XLA Ops:
  9.5 47.6 %all-gather = bf16[2048,192]{0,1:T(8,128)(2,1)S(1)} all-gather(bf16[128,192]{0,1:T(8,128)(2,1)} %param.17), channel_id=2, replica_groups=mesh['dp'=2,'row'=4,'col'=4] {'col','row'}, dimensions={0}, use_global_device_ids=true | all-gather | bytes 835584 | tf_op jit(solution)/shard_map/all_gather | solution.py:49
  60.2 6.9 %all-gather.5 = f32[4,192,6]{1,2,0:T(8,128)S(1)} all-gather(f32[1,192,6]{1,2,0:T(8,128)S(1)} %bitcast.211), channel_id=1, replica_groups=mesh['dp'=2,'row'=4,'col'=4] {'row'}, dimensions={0}, use_global_device_ids=true | all-gather | bytes 23040 | tf_op jit(solution)/shard_map/all_gather | solution.py:130
  69.0 13.3 %all_gather.51 = bf16[768,576]{1,0:T(8,128)(2,1)S(1)} all-gather(bf16[192,576]{1,0:T(8,128)(2,1)S(1)} %copy-done.18), channel_id=1, replica_groups=mesh['dp'=2,'row'=4,'col'=4] {'row'}, dimensions={0}, use_global_device_ids=true | all-gather | bytes 1105920 | tf_op jit(solution)/shard_map/all_gather | solution.py:129
  85.5 43.6 %all-gather.2 = bf16[2048,192]{0,1:T(8,128)(2,1)S(1)} all-gather(bf16[128,192]{0,1:T(8,128)(2,1)S(1)} %copy-done.33), channel_id=4, replica_groups=mesh['dp'=2,'row'=4,'col'=4] {'col','row'}, dimensions={0}, use_global_device_ids=true | all-gather | bytes 835584 | tf_op jit(solution)/shard_map/all_gather | solution.py:49
  131.5 4.1 fusion.73
  139.4 16.6 %all_gather.52 = bf16[512,768]{0,1:T(8,128)(2,1)} all-gather(bf16[512,192]{0,1:T(8,128)(2,1)S(1)} %bitcast.197), channel_id=1, replica_groups=mesh['dp'=2,'row'=4,'col'=4] {'col'}, dimensions={1}, use_global_device_ids=true | all-gather | bytes 983040 | tf_op jit(solution)/shard_map/all_gather | solution.py:164
  156.0 3.8 copy.219
  159.8 3.1 reshape.253
  162.9 2.6 fusion.70
  168.0 3.8 multiply_convert_fusion.1
  171.8 4.2 convert_reduce_fusion
  182.6 12.3 %reduce-scatter.12.cloned.1.call-done = bf16[128,192]{1,0:T(8,128)(2,1)} async-done(((bf16[512,192]{1,0:T(8,128)(2,1)}), bf16[128,192]{1,0:T(8,128)(2,1)}) %reduce-scatter.12.cloned.1.call-update) | async-done | bytes 49168 | tf_op jit(solution)/shard_map/reduce_scatter | solution.py:173
  195.9 44.8 %all-gather.3 = bf16[2048,192]{0,1:T(8,128)(2,1)} all-gather(bf16[128,192]{0,1:T(8,128)(2,1)S(1)} %copy.201), channel_id=5, replica_groups=mesh['dp'=2,'row'=4,'col'=4] {'col','row'}, dimensions={0}, use_global_device_ids=true | all-gather | bytes 835584 | tf_op jit(solution)/shard_map/all_gather | solution.py:49
  244.6 3.0 copy.174
  260.4 15.3 %all-reduce.7.cloned.1.call-done = (bf16[192,192]{0,1:T(8,128)(2,1)}, bf16[192,576]{1,0:T(8,128)(2,1)}, bf16[192,768]{1,0:T(8,128)(2,1)}, bf16[768,192]{0,1:T(8,128)(2,1)}) async-done(((bf16[192,192]{0,1:T(8,128)(2,1)}, bf16[192,576]{1,0:T(8,128)(2,1)}, bf16[192,768]{1,0:T(8,128)(2,1)}, bf16[768,192]{0,1:T(8,128)(2,1)}), (bf16[192,192]{0,1:T(8,128)(2,1)}, bf16[192,576]{1,0:T(8,128)(2,1)}, ...) | async-done | bytes 884752 | tf_op jit(solution)/shard_map/psum | solution.py:213
  281.2 13.6 %all_to_all.10 = bf16[4,192,384]{2,1,0:T(8,128)(2,1)S(1)} all-to-all(bf16[4,192,384]{2,1,0:T(8,128)(2,1)S(1)} %fusion.34), channel_id=1, replica_groups=mesh['dp'=2,'row'=4,'col'=4] {'row'}, dimensions={0} | all-to-all | bytes 1179648 | tf_op jit(solution)/shard_map/all_to_all | solution.py:235
  303.0 83.8 %all-gather.20.cloned.1.call-done = bf16[6144,768]{1,0:T(8,128)(2,1)} async-done(((bf16[768,768]{1,0:T(8,128)(2,1)}), bf16[6144,768]{1,0:T(8,128)(2,1)}) %all-gather.20.cloned.1.call-update) | async-done | bytes 9437200 | tf_op jit(solution)/shard_map/all_gather | solution.py:238
  386.7 5.7 %reduce_sum.204 = bf16[768,768]{1,0:T(8,128)(2,1)S(1)} reduce(bf16[8,768,768]{2,1,0:T(8,128)(2,1)} %bitcast.183, bf16[]{:T(256)} %constant.27.clone.1), dimensions={0}, to_apply=%region_31.32 | reduce | flops 4128768 | bytes 10616834 | tf_op jit(solution)/shard_map/reduce_sum | solution.py:237
  397.0 2.9 multiply_add_fusion.3
  403.6 6.3 %fusion.18 = bf16[768,384]{1,0:T(8,128)(2,1)} fusion(bf16[768,384]{1,0:T(8,128)(2,1)S(1)} %bitcast.190, f32[768,768]{1,0:T(8,128)} %multiply_add_fusion.4, f32[768,768]{1,0:T(8,128)} %multiply_add_fusion.1, f32[]{:T(128)S(6)} %rsqrt.28), kind=kOutput, calls=%fused_computation.51 | convolution fusion | flops 1363968000 | bytes 5898244 | tf_op jit(solution)/shard_map/dot_general | solution.py:63
  409.9 3.8 all-to-all-start.1
  418.4 4.5 all-to-all-done.1
  430.2 9.8 %all-reduce.2 = (f32[128,1]{0,1:T(1,128)S(1)}, f32[128,1]{0,1:T(1,128)S(1)}) all-reduce(f32[128,1]{0,1:T(1,128)S(1)} %bitcast.223, f32[128,1]{0,1:T(1,128)S(1)} %bitcast.224), channel_id=1, replica_groups=mesh['dp'=2,'row'=4,'col'=4] {'row'}, use_global_device_ids=true, to_apply=%region_15.16 | all-reduce | flops 256 | bytes 2048 | tf_op jit(solution)/shard_map/psum | solution.py:271
  442.1 14.5 %psum.71 = f32[6,192]{1,0:T(8,128)S(1)} all-reduce(f32[6,192]{1,0:T(8,128)S(1)} %stack.58), channel_id=1, replica_groups=mesh['dp'=2,'row'=4,'col'=4] {'dp','col'}, use_global_device_ids=true, to_apply=%region_30.31 | all-reduce | flops 1152 | bytes 9216 | tf_op jit(solution)/shard_map/psum | solution.py:291
  (211 shorter events, 85.8 us)
Async XLA Ops:
  7.2 148.8 %all-gather.18.cloned.1.call-start = ((), (), s32[]{:S(2)}) async-start(), calls=%async_computation.8 | async-start | bytes 1671168 | tf_op jit(solution)/shard_map/all_gather | solution.py:49
  7.9 160.1 %all-gather.12.cloned.1.call-start = ((), (), s32[]{:S(2)}) async-start(), calls=%async_computation.5 | async-start | bytes 1474560 | tf_op jit(solution)/shard_map/all_gather | solution.py:132
  8.7 163.1 %all-gather.14.cloned.1.call-start = ((), (), s32[]{:S(2)}) async-start(), calls=%async_computation.6 | async-start | bytes 1474560 | tf_op jit(solution)/shard_map/all_gather | solution.py:135
  9.4 185.5 %reduce-scatter.12.cloned.1.call-start = ((), (), s32[]{:S(2)}) async-start(), calls=%async_computation.11 | async-start | bytes 327680 | tf_op jit(solution)/shard_map/reduce_scatter | solution.py:173
  137.9 21.9 %copy-start.1 = (bf16[3,512,512]{1,2,0:T(8,128)(2,1)}, bf16[3,512,512]{1,2,0:T(8,128)(2,1)S(1)}, u32[]{:S(2)}) copy-start(bf16[3,512,512]{1,2,0:T(8,128)(2,1)S(1)} %fusion.19) | copy-start | bytes 4718596
  178.2 97.5 %all-reduce.7.cloned.1.call-start = ((), (), s32[]{:S(2)}) async-start(), calls=%async_computation.13 | async-start | bytes 1867776 | tf_op jit(solution)/shard_map/psum | solution.py:213
  260.1 17.7 %copy-start.25 = (f32[192,768]{1,0:T(8,128)S(1)}, f32[192,768]{1,0:T(8,128)}, u32[]{:S(2)}) copy-start(f32[192,768]{1,0:T(8,128)} %param.29) | copy-start | bytes 1769476
  260.2 126.6 %all-gather.20.cloned.1.call-start = ((), (), s32[]{:S(2)}) async-start(), calls=%async_computation.9 | async-start | bytes 10616832 | tf_op jit(solution)/shard_map/all_gather | solution.py:238
  296.6 120.7 %reduce-scatter.10.cloned.1.call-start = ((), (), s32[]{:S(2)}) async-start(), calls=%async_computation.10 | async-start | bytes 327680 | tf_op jit(solution)/shard_map/reduce_scatter | solution.py:262
  300.5 128.6 %reduce-scatter.14.cloned.1.call-start = ((), (), s32[]{:S(2)}) async-start(), calls=%async_computation.12 | async-start | bytes 327680 | tf_op jit(solution)/shard_map/reduce_scatter | solution.py:266
  409.9 13.9 %copy-start.41 = (f32[576]{0:T(1024)S(1)}, f32[576]{0:T(1024)}, u32[]{:S(2)}) copy-start(f32[576]{0:T(1024)} %param.24) | copy-start | bytes 6916
  409.9 13.9 %copy-start.42 = (f32[576]{0:T(1024)S(1)}, f32[576]{0:T(1024)}, u32[]{:S(2)}) copy-start(f32[576]{0:T(1024)} %param.31) | copy-start | bytes 6916
  409.9 16.3 %copy-start.32 = (bf16[128,192]{1,0:T(8,128)(2,1)S(1)}, bf16[128,192]{1,0:T(8,128)(2,1)}, u32[]{:S(2)}) copy-start(bf16[128,192]{1,0:T(8,128)(2,1)} %reduce-scatter.12.cloned.1.call-done) | copy-start | bytes 147460
  409.9 16.4 %copy-start.44 = (f32[768]{0:T(1024)S(1)}, f32[768]{0:T(1024)}, u32[]{:S(2)}) copy-start(f32[768]{0:T(1024)} %param.25) | copy-start | bytes 9220
  409.9 16.4 %copy-start.45 = (f32[768]{0:T(1024)S(1)}, f32[768]{0:T(1024)}, u32[]{:S(2)}) copy-start(f32[768]{0:T(1024)} %param.32) | copy-start | bytes 9220
  409.9 46.7 %copy-start.39 = (f32[6,192]{1,0:T(8,128)S(1)}, f32[6,192]{1,0:T(8,128)}, u32[]{:S(2)}) copy-start(f32[6,192]{1,0:T(8,128)} %param.33) | copy-start | bytes 13828
  409.9 13.0 %all-to-all-start.1 = ((bf16[4,192,384]{2,1,0:T(8,128)(2,1)}), bf16[4,192,384]{2,1,0:T(8,128)(2,1)S(1)}, u32[]{:S(2)}, u32[]{:S(2)}) async-start(bf16[4,192,384]{2,1,0:T(8,128)(2,1)} %bitcast.51), calls=%async_computation.1 | async-start | bytes 1179648 | tf_op jit(solution)/shard_map/all_to_all | solution.py:244
  413.7 43.6 %copy-start.29 = (bf16[192,192]{0,1:T(8,128)(2,1)S(1)}, bf16[192,192]{0,1:T(8,128)(2,1)}, u32[]{:S(2)}) copy-start(bf16[192,192]{0,1:T(8,128)(2,1)} %get-tuple-element.180) | copy-start | bytes 221188
  413.7 44.4 %copy-start.23 = (f32[192,192]{0,1:T(8,128)S(1)}, f32[192,192]{0,1:T(8,128)}, u32[]{:S(2)}) copy-start(f32[192,192]{0,1:T(8,128)} %get-tuple-element.207) | copy-start | bytes 442372
  413.7 45.2 %all-gather.16.cloned.1.call-start = ((), (), s32[]{:S(2)}) async-start(), calls=%async_computation.7 | async-start | bytes 1769472 | tf_op jit(solution)/shard_map/all_gather | solution.py:251
  417.3 42.6 %copy-start.46 = (f32[576]{0:T(1024)}, f32[576]{0:T(1024)S(1)}, u32[]{:S(2)}) copy-start(f32[576]{0:T(1024)S(1)} %get-tuple-element.178) | copy-start | bytes 6916
  417.3 42.6 %copy-start.47 = (f32[768]{0:T(1024)}, f32[768]{0:T(1024)S(1)}, u32[]{:S(2)}) copy-start(f32[768]{0:T(1024)S(1)} %get-tuple-element.179) | copy-start | bytes 9220
  423.8 36.9 %copy-start.19 = (bf16[192,576]{1,0:T(8,128)(2,1)S(1)}, bf16[192,576]{1,0:T(8,128)(2,1)}, u32[]{:S(2)}) copy-start(bf16[192,576]{1,0:T(8,128)(2,1)} %param.20) | copy-start | bytes 663556
  440.1 22.5 %copy-start.13 = (bf16[192,768]{1,0:T(8,128)(2,1)S(1)}, bf16[192,768]{1,0:T(8,128)(2,1)}, u32[]{:S(2)}) copy-start(bf16[192,768]{1,0:T(8,128)(2,1)} %param.22) | copy-start | bytes 884740
  (35 other events, 118.4 us)
Sparse Core Ops, SparseCore 0:
  10.8 64.3 all-gather.17
  77.0 32.7 all-gather.11
  111.6 27.0 all-gather.13
  178.3 16.5 reduce-scatter.11
  260.3 15.2 all-reduce.6
  296.7 89.9 all-gather.19
  389.6 18.3 reduce-scatter.9
  410.8 18.2 reduce-scatter.13
  431.2 7.3 all-gather.15
